TPU v7x, 32 devices: a whole 2x2x4 slice. The times are simulated.
32 devices in a mesh: groups: 2 (over y), ctx: 4 (over z), heads: 4 (over x, core).
Axes of the slice: x: 2, y: 2, z: 4, core: 2. Of those that a mesh axis runs over, the one named last changes fastest.
Arguments:
- queries: bfloat16 [2048, 4096], P(('groups', 'ctx'), 'heads'), parts along dimension 0
- keys: bfloat16 [2048, 1024], P(('groups', 'ctx'), 'heads'), parts along dimension 0
- values: bfloat16 [2048, 1024], P(('groups', 'ctx'), 'heads'), parts along dimension 0, may hold values from -6 to 6
- conv_kernel: float32 [32, 6, 11], P('heads')
- head_mix: float32 [8, 4, 4], P('heads')
- norm_gain: float32 [4096], P('heads'), may hold values from 0.5 to 1.5
- bounds: int32 [4], P('groups'), parts along dimension 0, may hold values from 0 to 1024, as said below
Outputs:
- attended: bfloat16 [2048, 4096], P(('groups', 'ctx'), 'heads'), parts along dimension 0
There are 2 independent parts, one for each index of `groups`. A program takes and returns all parts, laid end to end along the dimension named above; an argument that names none is the same for every part. Nothing has to cross between parts.
Inputs may be any that keep to these rules, and one draw needn't show every extreme that they name: bounds[0] < bounds[1], and bounds[1] >= 512.
All inputs are finite; a program needn't handle non-finite values.
Results may differ from a plain program's by a relative error of at most 0.0045.
Values may be sent and summed in bfloat16 or wider, within the bound.
No kernel may reach another device: no remote copies, remote signals or barrier semaphores. Data moves between devices by JAX's collectives and lax.ppermute only.
A program may use at most 64 MiB of HBM per device.

v0:
```python
import jax
import jax.numpy as jnp
from jax import lax
from jax.sharding import PartitionSpec as P

NEG_FILL = -1e30
EPSILON = 1e-06


def from_behind(value, axis, steps):
    count = lax.axis_size(axis)
    leading, last = (max(0, -steps), min(count, count - steps))
    return lax.ppermute(value, axis, [(source, source + steps) for source in range(leading, last)])


def conv_scores(zeroed, kernel, out_rows, out_cols, q_edge, k_edge):
    summed = jnp.zeros(zeroed.shape[:2] + (out_rows, out_cols), jnp.float32)
    for tap_row in range(kernel.shape[2]):
        for tap_col in range(kernel.shape[3]):
            summed = (
                summed
                + kernel[:, :, tap_row, tap_col][:, :, None, None]
                * zeroed[
                    :,
                    :,
                    q_edge - tap_row : q_edge - tap_row + out_rows,
                    2 * k_edge - tap_col : 2 * k_edge - tap_col + out_cols,
                ]
            )
    return summed


def per_device(queries, keys, values, conv_kernel, head_mix, norm_gain, bounds):
    num_rows = queries.shape[0]
    kv_local = head_mix.shape[0]
    heads_per_group = head_mix.shape[1]
    head_width = keys.shape[1] // kv_local
    q_taps = conv_kernel.shape[1]
    k_taps = conv_kernel.shape[2]
    q_edge = q_taps - 1
    k_edge = k_taps // 2
    score_scale = head_width ** (-0.5)
    ctx_size = lax.axis_size("ctx")
    row_first = lax.axis_index("ctx") * num_rows
    start_row = bounds[0]
    end_row = bounds[1]
    prior_rows = from_behind(queries[num_rows - q_edge :], "ctx", 1)
    query_ext = jnp.concatenate([prior_rows, queries], 0).reshape(
        num_rows + q_edge, kv_local, heads_per_group, head_width
    )
    kernel = conv_kernel.reshape(kv_local, heads_per_group, q_taps, k_taps)
    seg_rows = query_ext.shape[0] - q_edge
    ext_pos = row_first - q_edge + jnp.arange(seg_rows + q_edge, dtype=jnp.int32)
    pos = row_first + jnp.arange(seg_rows, dtype=jnp.int32)
    live = (pos >= start_row) & (pos < end_row)
    segments = ((query_ext, ext_pos, pos, live),)

    def attend(carry_state, segment, key_block, value_block, key_first):
        seg_queries, row_ext_pos, row_pos, row_live = segment
        seg_rows = row_pos.shape[0]
        run_max, run_sum, run_acc = carry_state
        key_count = value_block.shape[0]
        raw_scores = (
            jnp.einsum("rgmd,kgd->gmrk", seg_queries, key_block, preferred_element_type=jnp.float32)
            * score_scale
        )
        key_ext_pos = key_first - k_edge + jnp.arange(key_count + 2 * k_edge, dtype=jnp.int32)
        zeroed = jnp.where(key_ext_pos[None, :] <= row_ext_pos[:, None], raw_scores, 0.0)
        mixed_scores = conv_scores(zeroed, kernel, seg_rows, key_count, q_edge, k_edge)
        key_pos = key_first + jnp.arange(key_count, dtype=jnp.int32)
        valid_mask = (key_pos[None, :] <= row_pos[:, None]) & row_live[:, None]
        block_max = jnp.max(jnp.where(valid_mask, mixed_scores, NEG_FILL), axis=-1)
        new_max = jnp.maximum(run_max, block_max)
        weights = jnp.where(valid_mask, jnp.exp(mixed_scores - new_max[..., None]), 0.0)
        factor = jnp.exp(run_max - new_max)
        new_sum = run_sum * factor + jnp.sum(weights, axis=-1)
        product = jnp.einsum(
            "gmrk,kgd->rgmd",
            weights.astype(jnp.bfloat16),
            value_block,
            preferred_element_type=jnp.float32,
        )
        new_acc = run_acc * jnp.transpose(factor, (2, 0, 1))[..., None] + product
        return (new_max, new_sum, new_acc)

    def guarded(carry_state, segment, key_block, value_block, key_first):
        return attend(carry_state, segment, key_block, value_block, key_first)

    def guarded_all(states, key_block, value_block, key_first):
        return tuple(
            (
                guarded(states[idx], segments[idx], key_block, value_block, key_first)
                for idx in range(len(segments))
            )
        )

    def fresh_state(segment):
        seg_rows = segment[2].shape[0]
        return (
            jnp.full((kv_local, heads_per_group, seg_rows), NEG_FILL, jnp.float32),
            jnp.zeros((kv_local, heads_per_group, seg_rows), jnp.float32),
            jnp.zeros((seg_rows, kv_local, heads_per_group, head_width), jnp.float32),
        )

    initial = tuple((fresh_state(segment) for segment in segments))
    boundary = jnp.concatenate([keys[:k_edge], keys[num_rows - k_edge :]], 0)
    edge_table = lax.all_gather(boundary, "ctx", axis=0, tiled=True)
    edge_table = edge_table.reshape(ctx_size, 2 * k_edge, kv_local * head_width)
    blank_rows = jnp.zeros((1, 2 * k_edge, kv_local * head_width), keys.dtype)
    padded_table = jnp.concatenate([blank_rows, edge_table, blank_rows], 0)
    key_piece = lax.all_gather(keys, "ctx", axis=0, tiled=True)
    value_piece = lax.all_gather(values, "ctx", axis=0, tiled=True)
    shards = key_piece.shape[0] // num_rows
    key_split = key_piece.reshape(shards, num_rows, kv_local, head_width)
    value_split = value_piece.reshape(shards, num_rows, kv_local, head_width)

    def per_shard(shard_pos, inner_state):
        lower_edge = lax.dynamic_index_in_dim(padded_table, shard_pos, 0, keepdims=False)[k_edge:]
        upper_edge = lax.dynamic_index_in_dim(padded_table, shard_pos + 2, 0, keepdims=False)[
            :k_edge
        ]
        middle_keys = lax.dynamic_index_in_dim(key_split, shard_pos, 0, keepdims=False)
        block_keys = jnp.concatenate(
            [
                lower_edge.reshape(k_edge, kv_local, head_width),
                middle_keys,
                upper_edge.reshape(k_edge, kv_local, head_width),
            ],
            0,
        )
        block_values = lax.dynamic_index_in_dim(value_split, shard_pos, 0, keepdims=False)
        return guarded_all(inner_state, block_keys, block_values, shard_pos * num_rows)

    final_states = lax.fori_loop(0, shards, per_shard, initial)
    run_max, run_sum, run_acc = final_states[0]
    row_live = segments[0][3]
    seg_rows = row_live.shape[0]
    divisor = jnp.where(row_live[None, None, :], run_sum, 1.0)
    probs_out = run_acc / jnp.transpose(divisor, (2, 0, 1))[..., None]
    blended = jnp.einsum("gab,rgbd->rgad", head_mix, probs_out, precision=lax.Precision.HIGHEST)
    mean_sq = jnp.mean(blended * blended, axis=-1, keepdims=True)
    normed = (
        blended
        * lax.rsqrt(mean_sq + EPSILON)
        * norm_gain.reshape(kv_local, heads_per_group, head_width)
    )
    result = jnp.where(row_live[:, None, None, None], normed, 0.0)
    return result.reshape(seg_rows, kv_local * heads_per_group * head_width).astype(jnp.bfloat16)


def solution(mesh):
    return jax.shard_map(
        per_device,
        mesh=mesh,
        in_specs=(
            P(("groups", "ctx"), "heads"),
            P(("groups", "ctx"), "heads"),
            P(("groups", "ctx"), "heads"),
            P("heads", None, None),
            P("heads", None, None),
            P("heads"),
            P("groups"),
        ),
        out_specs=P(("groups", "ctx"), "heads"),
        check_vma=False,
    )
```

profile of v0, /device:TPU:0, one launch (start us, length us, event | category | flops | bytes accessed | tf_op | source)
XLA Modules:
  0.0 266.3 jit_solution(12256957341839974469)
XLA Ops:
  0.0 0.8 slice.1361
  0.8 4.9 %collective-permute-start = (bf16[5,1024]{1,0:T(8,128)(2,1)S(1)}, bf16[5,1024]{1,0:T(8,128)(2,1)S(1)}, u32[]{:S(2)}, u32[]{:S(2)}) collective-permute-start(bf16[5,1024]{1,0:T(8,128)(2,1)S(1)} %slice.1361), channel_id=1, source_target_pairs={{0,4},{4,8},{8,12},{1,5},{5,9},{9,13},{2,6},{6,10},{10,14},{3,7},{... | collective-permute-start | bytes 30728 | tf_op jit(solution)/shard_map/ppermute | solution.py:13
  5.8 0.7 fusion.89
  6.5 16.0 %all_gather.10 = bf16[1024,256]{1,0:T(8,128)(2,1)S(1)} all-gather(bf16[256,256]{1,0:T(8,128)(2,1)} %param.10), channel_id=1, replica_groups=mesh['groups'=2,'ctx'=4,'heads'=4] {'ctx'}, dimensions={0}, use_global_device_ids=true | all-gather | bytes 655360 | tf_op jit(solution)/shard_map/all_gather | solution.py:111
  22.4 13.1 %all-gather = bf16[4,10,256]{2,1,0:T(8,128)(2,1)S(1)} all-gather(bf16[1,10,256]{2,1,0:T(8,128)(2,1)S(1)} %maximum_bitcast_fusion.2), channel_id=1, replica_groups=mesh['groups'=2,'ctx'=4,'heads'=4] {'ctx'}, dimensions={0}, use_global_device_ids=true | all-gather | bytes 25600 | tf_op jit(solution)/shard_map/all_gather | solution.py:107
  35.6 1.3 fusion.90
  36.9 14.9 %all_gather.11 = bf16[1024,256]{1,0:T(8,128)(2,1)S(1)} all-gather(bf16[256,256]{1,0:T(8,128)(2,1)} %param.11), channel_id=1, replica_groups=mesh['groups'=2,'ctx'=4,'heads'=4] {'ctx'}, dimensions={0}, use_global_device_ids=true | all-gather | bytes 655360 | tf_op jit(solution)/shard_map/all_gather | solution.py:112
  51.8 1.7 compare_and_fusion.2
  53.6 0.9 reshape.80
  54.5 0.9 reshape.82
  55.7 0.3 reshape.81
  56.0 0.9 copy.34
  56.9 201.9 %while.22 = (s32[]{:T(128)}, f32[2,4,256]{2,1,0:T(4,128)S(1)}, f32[2,4,256]{2,1,0:T(4,128)S(1)}, f32[256,2,4,128]{0,3,2,1:T(8,128)}, f32[2,4,6,11]{1,0,3,2:T(2,1...) while((s32[]{:T(128)}, f32[2,4,256]{2,1,0:T(4,128)S(1)}, ...), condition=%wide.region_3.4_spmd.clone.clone.clone, body=%wide.region_0.3_spmd.clone.clone.clone.sunk | while | flops 351798912 | bytes 160064880 | solution.py:134
  56.9 1.2 constant_dynamic-slice_fusion.3
  58.0 0.7 copy.51
  58.9 1.9 bitcast_select_fusion.2
  60.7 1.2 compare_and_fusion.5
  62.1 0.7 slice_bitcast_fusion.70
  62.8 0.7 slice_bitcast_fusion.71
  63.4 0.7 slice_bitcast_fusion.72
  64.1 0.6 slice_bitcast_fusion.73
  64.7 38.1 %select_reduce_fusion.2 = (f32[2,4,256]{2,1,0:T(4,128)S(1)}, f32[2,4,256,256]{3,2,1,0:T(8,128)}) fusion(pred[256,256]{1,0:T(8,128)(4,1)S(1)} %compare_and_fusion.6, f32[2,4,261,266]{3,2,1,0:T(8,128)S(1)} %bitcast_select_fusion.2, f32[2,4]{1,0:T(2,128)S(1)} %get-tuple-element.735, f32[2,4]{1,0:T(2,128)S(1)} %get-tuple-element.736, ...), kind=kLoop, calls=%fused_computation.136.clone.1 | loop fusion | flops 69728256 | bytes 140585024 | tf_op jit(solution)/shard_map/while/body/eval_jaxpr/reduce_max | solution.py:72
  103.0 3.3 %fusion.106 = f32[256,2,4,128]{0,3,2,1:T(8,128)} fusion(f32[2,4,256,256]{3,2,1,0:T(8,128)} %get-tuple-element.803, f32[256,2,4,128]{0,3,2,1:T(8,128)} %get-tuple-element.829, f32[2,4,256]{2,1,0:T(4,128)S(1)} %get-tuple-element.847, pred[256,256]{1,0:T(8,128)(4,1)S(1)} %compare_and_fusion.6, f32[256,2,4]{0,2,1:T(4,128)S(1)} %get-tuple-element.804, ...), kind=kOutput, calls=%fused_computation.140.clone.1 | convolution fusion | flops 136577024 | bytes 4407297 | tf_op jit(solution)/shard_map/while/body/eval_jaxpr/gmrk,kgd->rgmd/dot_general | solution.py:77
  106.3 0.7 fusion.104
  107.2 1.2 constant_dynamic-slice_fusion.3
  108.3 0.7 copy.51
  109.2 1.9 bitcast_select_fusion.2
  111.0 1.2 compare_and_fusion.5
  112.4 0.7 slice_bitcast_fusion.70
  113.1 0.7 slice_bitcast_fusion.71
  113.7 0.7 slice_bitcast_fusion.72
  114.4 0.6 slice_bitcast_fusion.73
  115.0 38.1 %select_reduce_fusion.2 = (f32[2,4,256]{2,1,0:T(4,128)S(1)}, f32[2,4,256,256]{3,2,1,0:T(8,128)}) fusion(pred[256,256]{1,0:T(8,128)(4,1)S(1)} %compare_and_fusion.6, f32[2,4,261,266]{3,2,1,0:T(8,128)S(1)} %bitcast_select_fusion.2, f32[2,4]{1,0:T(2,128)S(1)} %get-tuple-element.735, f32[2,4]{1,0:T(2,128)S(1)} %get-tuple-element.736, ...), kind=kLoop, calls=%fused_computation.136.clone.1 | loop fusion | flops 69728256 | bytes 140585024 | tf_op jit(solution)/shard_map/while/body/eval_jaxpr/reduce_max | solution.py:72
  153.3 3.6 %fusion.106 = f32[256,2,4,128]{0,3,2,1:T(8,128)} fusion(f32[2,4,256,256]{3,2,1,0:T(8,128)} %get-tuple-element.803, f32[256,2,4,128]{0,3,2,1:T(8,128)} %get-tuple-element.829, f32[2,4,256]{2,1,0:T(4,128)S(1)} %get-tuple-element.847, pred[256,256]{1,0:T(8,128)(4,1)S(1)} %compare_and_fusion.6, f32[256,2,4]{0,2,1:T(4,128)S(1)} %get-tuple-element.804, ...), kind=kOutput, calls=%fused_computation.140.clone.1 | convolution fusion | flops 136577024 | bytes 4407297 | tf_op jit(solution)/shard_map/while/body/eval_jaxpr/gmrk,kgd->rgmd/dot_general | solution.py:77
  156.9 0.7 fusion.104
  157.7 1.2 constant_dynamic-slice_fusion.3
  158.9 0.7 copy.51
  159.7 1.9 bitcast_select_fusion.2
  161.6 1.2 compare_and_fusion.5
  163.0 0.7 slice_bitcast_fusion.70
  163.6 0.7 slice_bitcast_fusion.71
  164.3 0.7 slice_bitcast_fusion.72
  165.0 0.6 slice_bitcast_fusion.73
  165.6 38.1 %select_reduce_fusion.2 = (f32[2,4,256]{2,1,0:T(4,128)S(1)}, f32[2,4,256,256]{3,2,1,0:T(8,128)}) fusion(pred[256,256]{1,0:T(8,128)(4,1)S(1)} %compare_and_fusion.6, f32[2,4,261,266]{3,2,1,0:T(8,128)S(1)} %bitcast_select_fusion.2, f32[2,4]{1,0:T(2,128)S(1)} %get-tuple-element.735, f32[2,4]{1,0:T(2,128)S(1)} %get-tuple-element.736, ...), kind=kLoop, calls=%fused_computation.136.clone.1 | loop fusion | flops 69728256 | bytes 140585024 | tf_op jit(solution)/shard_map/while/body/eval_jaxpr/reduce_max | solution.py:72
  203.8 3.6 %fusion.106 = f32[256,2,4,128]{0,3,2,1:T(8,128)} fusion(f32[2,4,256,256]{3,2,1,0:T(8,128)} %get-tuple-element.803, f32[256,2,4,128]{0,3,2,1:T(8,128)} %get-tuple-element.829, f32[2,4,256]{2,1,0:T(4,128)S(1)} %get-tuple-element.847, pred[256,256]{1,0:T(8,128)(4,1)S(1)} %compare_and_fusion.6, f32[256,2,4]{0,2,1:T(4,128)S(1)} %get-tuple-element.804, ...), kind=kOutput, calls=%fused_computation.140.clone.1 | convolution fusion | flops 136577024 | bytes 4407297 | tf_op jit(solution)/shard_map/while/body/eval_jaxpr/gmrk,kgd->rgmd/dot_general | solution.py:77
  207.4 0.7 fusion.104
  208.3 1.2 constant_dynamic-slice_fusion.3
  209.5 0.7 copy.51
  210.3 1.9 bitcast_select_fusion.2
  212.1 1.2 compare_and_fusion.5
  213.5 0.7 slice_bitcast_fusion.70
  214.2 0.7 slice_bitcast_fusion.71
  214.9 0.7 slice_bitcast_fusion.72
  215.5 0.6 slice_bitcast_fusion.73
  216.1 38.1 %select_reduce_fusion.2 = (f32[2,4,256]{2,1,0:T(4,128)S(1)}, f32[2,4,256,256]{3,2,1,0:T(8,128)}) fusion(pred[256,256]{1,0:T(8,128)(4,1)S(1)} %compare_and_fusion.6, f32[2,4,261,266]{3,2,1,0:T(8,128)S(1)} %bitcast_select_fusion.2, f32[2,4]{1,0:T(2,128)S(1)} %get-tuple-element.735, f32[2,4]{1,0:T(2,128)S(1)} %get-tuple-element.736, ...), kind=kLoop, calls=%fused_computation.136.clone.1 | loop fusion | flops 69728256 | bytes 140585024 | tf_op jit(solution)/shard_map/while/body/eval_jaxpr/reduce_max | solution.py:72
  254.4 3.6 %fusion.106 = f32[256,2,4,128]{0,3,2,1:T(8,128)} fusion(f32[2,4,256,256]{3,2,1,0:T(8,128)} %get-tuple-element.803, f32[256,2,4,128]{0,3,2,1:T(8,128)} %get-tuple-element.829, f32[2,4,256]{2,1,0:T(4,128)S(1)} %get-tuple-element.847, pred[256,256]{1,0:T(8,128)(4,1)S(1)} %compare_and_fusion.6, f32[256,2,4]{0,2,1:T(4,128)S(1)} %get-tuple-element.804, ...), kind=kOutput, calls=%fused_computation.140.clone.1 | convolution fusion | flops 136577024 | bytes 4407297 | tf_op jit(solution)/shard_map/while/body/eval_jaxpr/gmrk,kgd->rgmd/dot_general | solution.py:77
  258.0 0.7 fusion.104
  258.8 0.6 select_bitcast_fusion
  259.4 1.3 broadcast_divide_fusion
  260.7 0.4 copy.36
  261.1 2.3 multiply_reduce_fusion
  263.5 1.5 select_convert_fusion
  265.0 0.3 copy.39
  265.3 1.0 copy.40
  (84 shorter events, 2.2 us)
Async XLA Ops:
  0.0 261.1 %copy-start = (f32[2,4,4]{2,1,0:T(4,128)S(1)}, f32[2,4,4]{2,1,0:T(4,128)}, u32[]{:S(2)}) copy-start(f32[2,4,4]{2,1,0:T(4,128)} %param.13) | copy-start | bytes 388
  0.0 55.5 %copy-start.2 = (bf16[256,1024]{1,0:T(8,128)(2,1)S(1)}, bf16[256,1024]{1,0:T(8,128)(2,1)}, u32[]{:S(2)}) copy-start(bf16[256,1024]{1,0:T(8,128)(2,1)} %param.9) | copy-start | bytes 1572868
  0.0 55.4 %copy-start.5 = (f32[8,6,11]{2,0,1:T(8,128)S(1)}, f32[8,6,11]{2,0,1:T(8,128)}, u32[]{:S(2)}) copy-start(f32[8,6,11]{2,0,1:T(8,128)} %param.12) | copy-start | bytes 6340
  0.8 54.7 %collective-permute-start = (bf16[5,1024]{1,0:T(8,128)(2,1)S(1)}, bf16[5,1024]{1,0:T(8,128)(2,1)S(1)}, u32[]{:S(2)}, u32[]{:S(2)}) collective-permute-start(bf16[5,1024]{1,0:T(8,128)(2,1)S(1)} %slice.1361), channel_id=1, source_target_pairs={{0,4},{4,8},{8,12},{1,5},{5,9},{9,13},{2,6},{6,10},{10,14},{3,7},{... | collective-permute-start | bytes 30728 | tf_op jit(solution)/shard_map/ppermute | solution.py:13
  56.9 2.0 copy-start.3
  103.0 3.4 %copy-start.1 = (f32[2,4,256,256]{3,2,1,0:T(8,128)S(1)}, f32[2,4,256,256]{3,2,1,0:T(8,128)}, u32[]{:S(2)}) copy-start(f32[2,4,256,256]{3,2,1,0:T(8,128)} %get-tuple-element.803) | copy-start | bytes 6291460 | tf_op jit(solution)/shard_map/while
  106.3 0.8 copy-start.4
  107.1 2.0 copy-start.3
  153.3 3.6 %copy-start.1 = (f32[2,4,256,256]{3,2,1,0:T(8,128)S(1)}, f32[2,4,256,256]{3,2,1,0:T(8,128)}, u32[]{:S(2)}) copy-start(f32[2,4,256,256]{3,2,1,0:T(8,128)} %get-tuple-element.803) | copy-start | bytes 6291460 | tf_op jit(solution)/shard_map/while
  156.9 0.8 copy-start.4
  157.7 2.0 copy-start.3
  203.8 3.6 %copy-start.1 = (f32[2,4,256,256]{3,2,1,0:T(8,128)S(1)}, f32[2,4,256,256]{3,2,1,0:T(8,128)}, u32[]{:S(2)}) copy-start(f32[2,4,256,256]{3,2,1,0:T(8,128)} %get-tuple-element.803) | copy-start | bytes 6291460 | tf_op jit(solution)/shard_map/while
  207.4 0.8 copy-start.4
  208.2 2.0 copy-start.3
  254.4 3.6 %copy-start.1 = (f32[2,4,256,256]{3,2,1,0:T(8,128)S(1)}, f32[2,4,256,256]{3,2,1,0:T(8,128)}, u32[]{:S(2)}) copy-start(f32[2,4,256,256]{3,2,1,0:T(8,128)} %get-tuple-element.803) | copy-start | bytes 6291460 | tf_op jit(solution)/shard_map/while
  258.0 0.8 copy-start.4
  260.7 2.8 %copy-start.6 = (pred[256]{0:T(512)(128)(4,1)S(1)}, pred[256]{0:T(512)(128)(4,1)}, u32[]{:S(2)}) copy-start(pred[256]{0:T(512)(128)(4,1)} %compare_and_fusion.2) | copy-start | bytes 772
  260.7 2.8 %copy-start.7 = (f32[1024]{0:T(1024)S(1)}, f32[1024]{0:T(1024)}, u32[]{:S(2)}) copy-start(f32[1024]{0:T(1024)} %param.14) | copy-start | bytes 12292
where the time goes:
time: 267 us; the launch traced here: 266 us
  other arithmetic  167 us (63%)
  blocking collectives  44 us (16%)
  local copies, waits for them, and re-layouts  26 us (10%)
  matrix products  23.9 us (9%)
  starting transfers between devices  4.95 us (2%)
    reduce_max x4, other arithmetic, attend(): block_max = jnp.max(jnp.where(valid_mask, mixed_scores, NEG_FILL), axis=-1)  152 us
    all_gather x1, blocking collectives, per_device(): key_piece = lax.all_gather(keys, 'ctx', axis=0, tiled=True)  16 us
    all_gather x1, blocking collectives, per_device(): value_piece = lax.all_gather(values, 'ctx', axis=0, tiled=True)  14.9 us
    dot_general x4, matrix products, attend(): jnp.einsum('gmrk,kgd->rgmd', weights.astype(jnp.bfloat16), value_block, p...  14.2 us
    all_gather x1, blocking collectives, per_device(): edge_table = lax.all_gather(boundary, 'ctx', axis=0, tiled=True)  13.1 us
    mul x16, local copies, waits for them, and re-layouts, conv_scores(): kernel[:, :, tap_row, tap_col][:, :, None, None]  10.4 us
    dot_general x4, matrix products, attend(): jnp.einsum('rgmd,kgd->gmrk', seg_queries, key_block, preferred_element_ty...  7.42 us
    and x5, other arithmetic, per_device(): live = (pos >= start_row) & (pos < end_row)  6.71 us
  transfers between devices with their start and end apart: 1, of which 0 were waited for; matrix products, arithmetic and copies ran while one was open for 2% of the time, Pallas kernels for 0%

commit v1 on v0

--- a/solution.py
+++ b/solution.py
@@ -5,6 +5,27 @@
 
 NEG_FILL = -1e30
 EPSILON = 1e-06
+
+
+def in_order(parts, dim):
+    shape = list(parts.shape[1:])
+    shape[dim] *= parts.shape[0]
+    return jnp.moveaxis(parts, 0, dim).reshape(shape)
+
+
+def collected_by_bits(x, axis):
+    length, index = (lax.axis_size(axis), lax.axis_index(axis))
+    blocks, distance = (x[None], 1)
+    while distance < length:
+        theirs = lax.ppermute(blocks, axis, [(i, i ^ distance) for i in range(length)])
+        low = index & distance == 0
+        blocks = jnp.concatenate([jnp.where(low, blocks, theirs), jnp.where(low, theirs, blocks)])
+        distance *= 2
+    return blocks
+
+
+def collect(x, axis, dim):
+    return in_order(collected_by_bits(x, axis), dim)
 
 
 def from_behind(value, axis, steps):
@@ -108,7 +129,7 @@
     edge_table = edge_table.reshape(ctx_size, 2 * k_edge, kv_local * head_width)
     blank_rows = jnp.zeros((1, 2 * k_edge, kv_local * head_width), keys.dtype)
     padded_table = jnp.concatenate([blank_rows, edge_table, blank_rows], 0)
-    key_piece = lax.all_gather(keys, "ctx", axis=0, tiled=True)
+    key_piece = collect(keys, "ctx", 0)
     value_piece = lax.all_gather(values, "ctx", axis=0, tiled=True)
     shards = key_piece.shape[0] // num_rows
     key_split = key_piece.reshape(shards, num_rows, kv_local, head_width)

time: 267 us -> 246 us (0.921)
  blocking collectives: 44 us -> 29.3 us
  other arithmetic: 167 us -> 159 us
  local copies, waits for them, and re-layouts: 26 us -> 22.7 us
  waiting for transfers between devices: 0.01 us -> 2.87 us
    all_gather x1 -> x0, blocking collectives: 16 us -> none  [per_device(): key_piece = lax.all_gather(keys, 'ctx', axis=0, tiled=True)]
    reduce_max x4, other arithmetic: 152 us -> 144 us  [attend(): block_max = jnp.max(jnp.where(valid_mask, mixed_scores, NEG_FILL), axis=-1)]
    mul x16, local copies, waits for them, and re-layouts: 10.4 us -> 4.95 us  [conv_scores(): kernel[:, :, tap_row, tap_col][:, :, None, None]]
    ppermute x0 -> x2, starting transfers between devices: none -> 5.07 us  [collected_by_bits(): lax.ppermute(blocks, axis, [(i, i ^ distance) for i in range(length)])]
    ppermute x1, starting transfers between devices: 4.95 us -> 1.91 us  [from_behind(): lax.ppermute(value, axis, [(source, source + steps) for source in range(l...]
    ppermute x0 -> x2, waiting for transfers between devices: none -> 2.87 us  [collected_by_bits(): lax.ppermute(blocks, axis, [(i, i ^ distance) for i in range(length)])]
  transfers between devices with their start and end apart: 1 -> 3, of which waited for: 0 -> 1; matrix products, arithmetic and copies ran while one was open for 2% -> 3% of each run, Pallas kernels for 0% -> 0%
where the time goes in v1:
time: 246 us
  other arithmetic  159 us (65%)
  blocking collectives  29.3 us (12%)
  matrix products  23.7 us (10%)
  local copies, waits for them, and re-layouts  22.7 us (9%)
  starting transfers between devices  6.98 us (3%)
  waiting for transfers between devices  2.87 us (1%)
    reduce_max x4, other arithmetic, attend(): block_max = jnp.max(jnp.where(valid_mask, mixed_scores, NEG_FILL), axis=-1)  144 us
    all_gather x1, blocking collectives, per_device(): value_piece = lax.all_gather(values, 'ctx', axis=0, tiled=True)  16.1 us
    dot_general x4, matrix products, attend(): jnp.einsum('gmrk,kgd->rgmd', weights.astype(jnp.bfloat16), value_block, p...  14.2 us
    all_gather x1, blocking collectives, per_device(): edge_table = lax.all_gather(boundary, 'ctx', axis=0, tiled=True)  13.2 us
    dot_general x4, matrix products, attend(): jnp.einsum('rgmd,kgd->gmrk', seg_queries, key_block, preferred_element_ty...  7.26 us
    and x5, other arithmetic, per_device(): live = (pos >= start_row) & (pos < end_row)  6.82 us
    ppermute x2, starting transfers between devices, collected_by_bits(): lax.ppermute(blocks, axis, [(i, i ^ distance) for i in range(length)])  5.07 us
    mul x16, local copies, waits for them, and re-layouts, conv_scores(): kernel[:, :, tap_row, tap_col][:, :, None, None]  4.95 us
  transfers between devices with their start and end apart: 3, of which 1 were waited for; matrix products, arithmetic and copies ran while one was open for 3% of the time, Pallas kernels for 0%

profile of v1, /device:TPU:0, one launch (start us, length us, event | category | flops | bytes accessed | tf_op | source)
XLA Modules:
  0.0 245.8 jit_solution(1284739310500842121)
XLA Ops:
  0.0 1.1 copy.35
  1.1 3.1 %collective-permute-start = (bf16[1,256,256]{1,2,0:T(8,128)(2,1)S(1)}, bf16[1,256,256]{1,2,0:T(8,128)(2,1)S(1)}, u32[]{:S(2)}, u32[]{:S(2)}) collective-permute-start(bf16[1,256,256]{1,2,0:T(8,128)(2,1)S(1)} %bitcast.207), channel_id=1, source_target_pairs={{0,4},{4,0},{8,12},{12,8},{1,5},{5,1},{9,13},{13,9},{2,6},{6,2},{1... | collective-permute-start | bytes 393224 | tf_op jit(solution)/shard_map/ppermute | solution.py:20
  4.2 0.7 slice.1361
  4.9 1.9 collective-permute-start.2
  6.8 0.7 fusion.89
  7.6 16.1 %all_gather.7 = bf16[1024,256]{1,0:T(8,128)(2,1)S(1)} all-gather(bf16[256,256]{1,0:T(8,128)(2,1)} %param.11), channel_id=1, replica_groups=mesh['groups'=2,'ctx'=4,'heads'=4] {'ctx'}, dimensions={0}, use_global_device_ids=true | all-gather | bytes 655360 | tf_op jit(solution)/shard_map/all_gather | solution.py:133
  23.7 13.2 %all-gather = bf16[4,10,256]{2,1,0:T(8,128)(2,1)S(1)} all-gather(bf16[1,10,256]{2,1,0:T(8,128)(2,1)S(1)} %maximum_bitcast_fusion.2), channel_id=1, replica_groups=mesh['groups'=2,'ctx'=4,'heads'=4] {'ctx'}, dimensions={0}, use_global_device_ids=true | all-gather | bytes 25600 | tf_op jit(solution)/shard_map/all_gather | solution.py:128
  37.0 1.9 collective-permute-start.1
  38.9 0.6 fusion.90
  39.6 1.7 compare_and_fusion.2
  41.3 0.9 reshape.78
  42.2 0.8 copy.36
  43.1 0.3 reshape.77
  43.4 0.9 copy.38
  44.3 2.9 %collective-permute-done.1 = bf16[2,256,256]{1,2,0:T(8,128)(2,1)S(1)} collective-permute-done((bf16[2,256,256]{1,2,0:T(8,128)(2,1)S(1)}, bf16[2,256,256]{1,2,0:T(8,128)(2,1)S(1)}, u32[]{:S(2)}, u32[]{:S(2)}) %collective-permute-start.1) | collective-permute-done | bytes 262176 | tf_op jit(solution)/shard_map/ppermute | solution.py:20
  47.2 190.9 %while.22 = (s32[]{:T(128)}, f32[2,4,256]{2,1,0:T(4,128)S(1)}, f32[2,4,256]{2,1,0:T(4,128)}, f32[256,2,4,128]{0,3,2,1:T(8,128)}, f32[2,4,6,11]{1,0,3,2:T(2,128)}...) while((s32[]{:T(128)}, f32[2,4,256]{2,1,0:T(4,128)S(1)}, ...), condition=%wide.region_3.4_spmd.clone.clone.clone, body=%wide.region_0.3_spmd.clone.clone.clone.sunk | while | flops 351798912 | bytes 164333328 | solution.py:155
  47.3 0.7 dynamic-slice_bitcast_fusion.3
  48.3 1.8 bitcast_select_fusion.2
  50.1 1.3 compare_and_fusion.5
  51.4 0.1 compare_and_fusion.6
  51.6 0.6 slice_bitcast_fusion.72
  52.2 0.6 slice_bitcast_fusion.73
  52.8 36.1 %select_reduce_fusion.2 = (f32[2,4,256]{2,1,0:T(4,128)S(1)}, f32[2,4,256,256]{3,2,1,0:T(8,128)}) fusion(pred[256,256]{1,0:T(8,128)(4,1)S(1)} %compare_and_fusion.6, f32[2,4,261,266]{3,2,1,0:T(8,128)S(1)} %bitcast_select_fusion.2, f32[2,4]{1,0:T(2,128)S(1)} %get-tuple-element.734, f32[2,4]{1,0:T(2,128)S(1)} %get-tuple-element.735, ...), kind=kLoop, calls=%fused_computation.136.clone.1 | loop fusion | flops 69728256 | bytes 140585024 | tf_op jit(solution)/shard_map/while/body/eval_jaxpr/reduce_max | solution.py:93
  88.9 1.0 constant_dynamic-slice_fusion.5
  90.1 3.3 %fusion.106 = f32[256,2,4,128]{0,3,2,1:T(8,128)} fusion(f32[2,4,256,256]{3,2,1,0:T(8,128)} %get-tuple-element.802, f32[256,2,4,128]{0,3,2,1:T(8,128)} %get-tuple-element.827, f32[2,4,256]{2,1,0:T(4,128)S(1)} %get-tuple-element.845, pred[256,256]{1,0:T(8,128)(4,1)S(1)} %compare_and_fusion.6, f32[256,2,4]{0,2,1:T(4,128)S(1)} %get-tuple-element.803, ...), kind=kOutput, calls=%fused_computation.140.clone.1 | convolution fusion | flops 136577024 | bytes 4407297 | tf_op jit(solution)/shard_map/while/body/eval_jaxpr/gmrk,kgd->rgmd/dot_general | solution.py:98
  93.4 0.7 fusion.104
  94.2 0.6 copy-done.7
  94.8 0.7 dynamic-slice_bitcast_fusion.3
  95.8 1.8 bitcast_select_fusion.2
  97.7 1.3 compare_and_fusion.5
  99.1 0.6 slice_bitcast_fusion.72
  99.7 0.6 slice_bitcast_fusion.73
  100.3 36.1 %select_reduce_fusion.2 = (f32[2,4,256]{2,1,0:T(4,128)S(1)}, f32[2,4,256,256]{3,2,1,0:T(8,128)}) fusion(pred[256,256]{1,0:T(8,128)(4,1)S(1)} %compare_and_fusion.6, f32[2,4,261,266]{3,2,1,0:T(8,128)S(1)} %bitcast_select_fusion.2, f32[2,4]{1,0:T(2,128)S(1)} %get-tuple-element.734, f32[2,4]{1,0:T(2,128)S(1)} %get-tuple-element.735, ...), kind=kLoop, calls=%fused_computation.136.clone.1 | loop fusion | flops 69728256 | bytes 140585024 | tf_op jit(solution)/shard_map/while/body/eval_jaxpr/reduce_max | solution.py:93
  136.4 1.0 constant_dynamic-slice_fusion.5
  137.6 3.6 %fusion.106 = f32[256,2,4,128]{0,3,2,1:T(8,128)} fusion(f32[2,4,256,256]{3,2,1,0:T(8,128)} %get-tuple-element.802, f32[256,2,4,128]{0,3,2,1:T(8,128)} %get-tuple-element.827, f32[2,4,256]{2,1,0:T(4,128)S(1)} %get-tuple-element.845, pred[256,256]{1,0:T(8,128)(4,1)S(1)} %compare_and_fusion.6, f32[256,2,4]{0,2,1:T(4,128)S(1)} %get-tuple-element.803, ...), kind=kOutput, calls=%fused_computation.140.clone.1 | convolution fusion | flops 136577024 | bytes 4407297 | tf_op jit(solution)/shard_map/while/body/eval_jaxpr/gmrk,kgd->rgmd/dot_general | solution.py:98
  141.2 0.7 fusion.104
  142.0 0.6 copy-done.7
  142.6 0.7 dynamic-slice_bitcast_fusion.3
  143.6 1.8 bitcast_select_fusion.2
  145.4 1.3 compare_and_fusion.5
  146.9 0.6 slice_bitcast_fusion.72
  147.5 0.6 slice_bitcast_fusion.73
  148.1 36.1 %select_reduce_fusion.2 = (f32[2,4,256]{2,1,0:T(4,128)S(1)}, f32[2,4,256,256]{3,2,1,0:T(8,128)}) fusion(pred[256,256]{1,0:T(8,128)(4,1)S(1)} %compare_and_fusion.6, f32[2,4,261,266]{3,2,1,0:T(8,128)S(1)} %bitcast_select_fusion.2, f32[2,4]{1,0:T(2,128)S(1)} %get-tuple-element.734, f32[2,4]{1,0:T(2,128)S(1)} %get-tuple-element.735, ...), kind=kLoop, calls=%fused_computation.136.clone.1 | loop fusion | flops 69728256 | bytes 140585024 | tf_op jit(solution)/shard_map/while/body/eval_jaxpr/reduce_max | solution.py:93
  184.2 1.0 constant_dynamic-slice_fusion.5
  185.4 3.6 %fusion.106 = f32[256,2,4,128]{0,3,2,1:T(8,128)} fusion(f32[2,4,256,256]{3,2,1,0:T(8,128)} %get-tuple-element.802, f32[256,2,4,128]{0,3,2,1:T(8,128)} %get-tuple-element.827, f32[2,4,256]{2,1,0:T(4,128)S(1)} %get-tuple-element.845, pred[256,256]{1,0:T(8,128)(4,1)S(1)} %compare_and_fusion.6, f32[256,2,4]{0,2,1:T(4,128)S(1)} %get-tuple-element.803, ...), kind=kOutput, calls=%fused_computation.140.clone.1 | convolution fusion | flops 136577024 | bytes 4407297 | tf_op jit(solution)/shard_map/while/body/eval_jaxpr/gmrk,kgd->rgmd/dot_general | solution.py:98
  189.0 0.7 fusion.104
  189.8 0.6 copy-done.7
  190.4 0.7 dynamic-slice_bitcast_fusion.3
  191.4 1.8 bitcast_select_fusion.2
  193.2 1.3 compare_and_fusion.5
  194.7 0.6 slice_bitcast_fusion.72
  195.3 0.6 slice_bitcast_fusion.73
  195.9 36.1 %select_reduce_fusion.2 = (f32[2,4,256]{2,1,0:T(4,128)S(1)}, f32[2,4,256,256]{3,2,1,0:T(8,128)}) fusion(pred[256,256]{1,0:T(8,128)(4,1)S(1)} %compare_and_fusion.6, f32[2,4,261,266]{3,2,1,0:T(8,128)S(1)} %bitcast_select_fusion.2, f32[2,4]{1,0:T(2,128)S(1)} %get-tuple-element.734, f32[2,4]{1,0:T(2,128)S(1)} %get-tuple-element.735, ...), kind=kLoop, calls=%fused_computation.136.clone.1 | loop fusion | flops 69728256 | bytes 140585024 | tf_op jit(solution)/shard_map/while/body/eval_jaxpr/reduce_max | solution.py:93
  232.0 1.0 constant_dynamic-slice_fusion.5
  233.1 3.6 %fusion.106 = f32[256,2,4,128]{0,3,2,1:T(8,128)} fusion(f32[2,4,256,256]{3,2,1,0:T(8,128)} %get-tuple-element.802, f32[256,2,4,128]{0,3,2,1:T(8,128)} %get-tuple-element.827, f32[2,4,256]{2,1,0:T(4,128)S(1)} %get-tuple-element.845, pred[256,256]{1,0:T(8,128)(4,1)S(1)} %compare_and_fusion.6, f32[256,2,4]{0,2,1:T(4,128)S(1)} %get-tuple-element.803, ...), kind=kOutput, calls=%fused_computation.140.clone.1 | convolution fusion | flops 136577024 | bytes 4407297 | tf_op jit(solution)/shard_map/while/body/eval_jaxpr/gmrk,kgd->rgmd/dot_general | solution.py:98
  236.7 0.7 fusion.104
  237.5 0.6 copy-done.7
  238.1 0.7 select_bitcast_fusion
  238.8 1.3 broadcast_divide_fusion
  240.2 0.4 copy.40
  240.6 2.3 multiply_reduce_fusion
  243.0 1.5 select_convert_fusion
  244.5 0.3 copy.43
  244.8 1.0 copy.44
  (137 shorter events, 2.7 us)
Async XLA Ops:
  0.0 240.6 %copy-start = (f32[2,4,4]{2,1,0:T(4,128)S(1)}, f32[2,4,4]{2,1,0:T(4,128)}, u32[]{:S(2)}) copy-start(f32[2,4,4]{2,1,0:T(4,128)} %param.13) | copy-start | bytes 388
  0.0 43.0 %copy-start.5 = (bf16[256,1024]{1,0:T(8,128)(2,1)S(1)}, bf16[256,1024]{1,0:T(8,128)(2,1)}, u32[]{:S(2)}) copy-start(bf16[256,1024]{1,0:T(8,128)(2,1)} %param.9) | copy-start | bytes 1572868
  0.0 38.9 %copy-start.13 = (s32[2]{0:T(128)S(1)}, s32[2]{0:T(128)}, u32[]{:S(2)}) copy-start(s32[2]{0:T(128)} %param.15) | copy-start | bytes 28
  0.0 42.2 %copy-start.10 = (f32[8,6,11]{2,0,1:T(8,128)S(1)}, f32[8,6,11]{2,0,1:T(8,128)}, u32[]{:S(2)}) copy-start(f32[8,6,11]{2,0,1:T(8,128)} %param.12) | copy-start | bytes 6340
  1.1 35.8 %collective-permute-start = (bf16[1,256,256]{1,2,0:T(8,128)(2,1)S(1)}, bf16[1,256,256]{1,2,0:T(8,128)(2,1)S(1)}, u32[]{:S(2)}, u32[]{:S(2)}) collective-permute-start(bf16[1,256,256]{1,2,0:T(8,128)(2,1)S(1)} %bitcast.207), channel_id=1, source_target_pairs={{0,4},{4,0},{8,12},{12,8},{1,5},{5,1},{9,13},{13,9},{2,6},{6,2},{1... | collective-permute-start | bytes 393224 | tf_op jit(solution)/shard_map/ppermute | solution.py:20
  4.9 38.1 %collective-permute-start.2 = (bf16[5,1024]{1,0:T(8,128)(2,1)S(1)}, bf16[5,1024]{1,0:T(8,128)(2,1)S(1)}, u32[]{:S(2)}, u32[]{:S(2)}) collective-permute-start(bf16[5,1024]{1,0:T(8,128)(2,1)S(1)} %slice.1361), channel_id=1, source_target_pairs={{0,4},{4,8},{8,12},{1,5},{5,9},{9,13},{2,6},{6,10},{10,14},{3,7},{... | collective-permute-start | bytes 30728 | tf_op jit(solution)/shard_map/ppermute | solution.py:34
  37.0 10.1 %collective-permute-start.1 = (bf16[2,256,256]{1,2,0:T(8,128)(2,1)S(1)}, bf16[2,256,256]{1,2,0:T(8,128)(2,1)S(1)}, u32[]{:S(2)}, u32[]{:S(2)}) collective-permute-start(bf16[2,256,256]{1,2,0:T(8,128)(2,1)S(1)} %pad_maximum_fusion.2), channel_id=1, source_target_pairs={{0,8},{4,12},{8,0},{12,4},{1,9},{5,13},{9,1},{13,5},{2,10},{6,14},... | collective-permute-start | bytes 786440 | tf_op jit(solution)/shard_map/ppermute | solution.py:20
  47.3 1.0 copy-start.2
  47.3 1.0 copy-start.8
  48.3 3.3 %copy-start.4 = (f32[2,4,6,11]{1,0,3,2:T(2,128)S(1)}, f32[2,4,6,11]{1,0,3,2:T(2,128)}, u32[]{:S(2)}) copy-start(f32[2,4,6,11]{1,0,3,2:T(2,128)} %get-tuple-element.848) | copy-start | bytes 6340 | tf_op jit(solution)/shard_map/while
  90.1 3.4 %copy-start.1 = (f32[2,4,256,256]{3,2,1,0:T(8,128)S(1)}, f32[2,4,256,256]{3,2,1,0:T(8,128)}, u32[]{:S(2)}) copy-start(f32[2,4,256,256]{3,2,1,0:T(8,128)} %get-tuple-element.802) | copy-start | bytes 6291460 | tf_op jit(solution)/shard_map/while
  93.4 0.8 copy-start.6
  93.4 1.4 copy-start.3
  93.4 1.4 copy-start.9
  94.2 0.6 copy-start.7
  94.8 1.0 copy-start.2
  94.8 1.0 copy-start.8
  95.8 3.3 %copy-start.4 = (f32[2,4,6,11]{1,0,3,2:T(2,128)S(1)}, f32[2,4,6,11]{1,0,3,2:T(2,128)}, u32[]{:S(2)}) copy-start(f32[2,4,6,11]{1,0,3,2:T(2,128)} %get-tuple-element.848) | copy-start | bytes 6340 | tf_op jit(solution)/shard_map/while
  137.6 3.6 %copy-start.1 = (f32[2,4,256,256]{3,2,1,0:T(8,128)S(1)}, f32[2,4,256,256]{3,2,1,0:T(8,128)}, u32[]{:S(2)}) copy-start(f32[2,4,256,256]{3,2,1,0:T(8,128)} %get-tuple-element.802) | copy-start | bytes 6291460 | tf_op jit(solution)/shard_map/while
  141.2 0.8 copy-start.6
  141.2 1.4 copy-start.3
  141.2 1.4 copy-start.9
  142.0 0.6 copy-start.7
  142.6 1.0 copy-start.2
  142.6 1.0 copy-start.8
  143.6 3.3 %copy-start.4 = (f32[2,4,6,11]{1,0,3,2:T(2,128)S(1)}, f32[2,4,6,11]{1,0,3,2:T(2,128)}, u32[]{:S(2)}) copy-start(f32[2,4,6,11]{1,0,3,2:T(2,128)} %get-tuple-element.848) | copy-start | bytes 6340 | tf_op jit(solution)/shard_map/while
  185.3 3.6 %copy-start.1 = (f32[2,4,256,256]{3,2,1,0:T(8,128)S(1)}, f32[2,4,256,256]{3,2,1,0:T(8,128)}, u32[]{:S(2)}) copy-start(f32[2,4,256,256]{3,2,1,0:T(8,128)} %get-tuple-element.802) | copy-start | bytes 6291460 | tf_op jit(solution)/shard_map/while
  189.0 0.8 copy-start.6
  189.0 1.4 copy-start.3
  189.0 1.4 copy-start.9
  189.7 0.6 copy-start.7
  190.4 1.0 copy-start.2
  190.4 1.0 copy-start.8
  191.3 3.3 %copy-start.4 = (f32[2,4,6,11]{1,0,3,2:T(2,128)S(1)}, f32[2,4,6,11]{1,0,3,2:T(2,128)}, u32[]{:S(2)}) copy-start(f32[2,4,6,11]{1,0,3,2:T(2,128)} %get-tuple-element.848) | copy-start | bytes 6340 | tf_op jit(solution)/shard_map/while
  233.1 3.6 %copy-start.1 = (f32[2,4,256,256]{3,2,1,0:T(8,128)S(1)}, f32[2,4,256,256]{3,2,1,0:T(8,128)}, u32[]{:S(2)}) copy-start(f32[2,4,256,256]{3,2,1,0:T(8,128)} %get-tuple-element.802) | copy-start | bytes 6291460 | tf_op jit(solution)/shard_map/while
  236.7 0.8 copy-start.6
  236.7 1.4 copy-start.3
  236.7 1.4 copy-start.9
  237.5 0.6 copy-start.7
  240.2 2.8 %copy-start.11 = (pred[256]{0:T(512)(128)(4,1)S(1)}, pred[256]{0:T(512)(128)(4,1)}, u32[]{:S(2)}) copy-start(pred[256]{0:T(512)(128)(4,1)} %compare_and_fusion.2) | copy-start | bytes 772
  240.2 2.8 %copy-start.12 = (f32[1024]{0:T(1024)S(1)}, f32[1024]{0:T(1024)}, u32[]{:S(2)}) copy-start(f32[1024]{0:T(1024)} %param.14) | copy-start | bytes 12292
